TPU v7x, 256 devices: a whole 4x4x8 slice. The times are simulated.
256 devices in a mesh: chain: 64 (over z, x, core), term: 4 (over y).
Axes of the slice: x: 4, y: 4, z: 8, core: 2. Of those that a mesh axis runs over, the one named last changes fastest.
Arguments:
- psi_guess: float32 [64, 8, 128, 128], P('chain'), may hold values from -6 to 6
- transfer_raw: float32 [64, 8, 128, 128], P('chain'), may hold values from -6 to 6
- left_env: float32 [64, 32, 8, 128, 128], P('chain', 'term'), may hold values from -0.75 to 0.75
- right_env: float32 [64, 32, 8, 128, 128], P('chain', 'term'), may hold values from -0.75 to 0.75
- block_sizes: int32 [64, 2, 8], P('chain'), may hold values from 64 to 128
Outputs:
- psi_out: float32 [64, 8, 128, 128], P('chain', 'term')
- energy: float32 [64], P('chain')
All inputs are finite; a program needn't handle non-finite values.
Results may differ from a plain program's by a relative error of at most 0.0003.
Values sent between devices are 32-bit elements; how exact they have to be, the bound alone decides.
No kernel may reach another device: no remote copies, remote signals or barrier semaphores. Data moves between devices by JAX's collectives and lax.ppermute only.
A program may use at most 128 MiB of HBM per device.

v0:
```python
import math
import jax
import jax.numpy as jnp
from jax import lax
from jax.sharding import PartitionSpec as P

ITERS = 4
precise = lax.Precision.HIGHEST
twist_scale = 0.22
shrink = 1.047
epsilon = 1e-06


def from_behind(value, axis, steps):
    count = lax.axis_size(axis)
    leading, last = (max(0, -steps), min(count, count - steps))
    return lax.ppermute(value, axis, [(source, source + steps) for source in range(leading, last)])


def transfer(raw_normal):
    block_len = raw_normal.shape[-1]
    identity = jnp.eye(block_len, dtype=jnp.float32)
    skewed = (raw_normal - jnp.swapaxes(raw_normal, -1, -2)) * (
        twist_scale / math.sqrt(2.0 * block_len)
    )
    return (identity + skewed) / shrink


def symmetric(raw_normal):
    return 0.5 * (raw_normal + jnp.swapaxes(raw_normal, -1, -2))


def sector_mask(sizes_pair, block_len):
    positions = jnp.arange(block_len, dtype=jnp.int32)
    row_live = (positions[None, :] < sizes_pair[0][:, None]).astype(jnp.float32)
    col_live = (positions[None, :] < sizes_pair[1][:, None]).astype(jnp.float32)
    return row_live[:, :, None] * col_live[:, None, :]


def local(psi_guess, transfer_raw, left_env, right_env, block_sizes):
    blocks = transfer(transfer_raw[0])
    sectors = blocks.shape[0]
    block_len = blocks.shape[-1]
    identity = jnp.broadcast_to(jnp.eye(block_len, dtype=jnp.float32), blocks.shape)
    position = lax.axis_index("chain")
    segments = lax.axis_size("chain")
    from_left, left_blocks = from_behind((left_env[0], blocks), "chain", 1)
    from_right, right_blocks = from_behind((right_env[0], blocks), "chain", -1)
    is_first = position == 0
    is_last = position == segments - 1
    prefix = jnp.where(is_first, identity, left_blocks)
    suffix = jnp.where(is_last, identity, right_blocks)
    left_sym = symmetric(jnp.where(is_first, left_env[0], from_left))
    right_sym = symmetric(jnp.where(is_last, right_env[0], from_right))
    live_mask = sector_mask(block_sizes[0], block_len)
    groups = lax.axis_size("term")
    owned = sectors // groups
    offset = lax.axis_index("term") * owned
    volume = float(sectors * block_len * block_len)
    partway = jnp.einsum("tkjl,klm->tkjm", left_sym, prefix, precision=precise)
    left_full = jnp.einsum("kji,tkjm->tkim", prefix, partway, precision=precise)
    partway = jnp.einsum("kij,tkjl->tkil", suffix, right_sym, precision=precise)
    right_full = jnp.einsum("tkil,kml->tkim", partway, suffix, precision=precise)

    def partial_term(vector):
        halfway = jnp.einsum("tkij,kjl->tkil", left_full, vector, precision=precise)
        return jnp.einsum("tkil,tklm->kim", halfway, right_full, precision=precise)

    def finish(summed):
        return live_mask * summed

    started = live_mask * psi_guess[0]
    start_norm = jnp.sqrt(jnp.sum(started * started) / volume + epsilon)
    vector = started / start_norm

    def apply_whole(direction):
        return finish(lax.psum(partial_term(direction), "term"))

    def mean_dot(first_arr, second_arr):
        return jnp.sum(first_arr * second_arr) / volume

    image = apply_whole(vector)
    energy = mean_dot(vector, image)
    for step_index in range(ITERS):
        residual = image - energy * vector
        res_norm = jnp.sqrt(mean_dot(residual, residual) + epsilon)
        along = mean_dot(residual, image) / res_norm
        unit_dir = residual / res_norm
        image_unit = apply_whole(unit_dir)
        curve = mean_dot(unit_dir, image_unit)
        gap_half = 0.5 * (curve - energy)
        lowest = 0.5 * (curve + energy) - jnp.sqrt(gap_half * gap_half + along * along)
        coef_b = lowest - energy
        combined = jnp.sqrt(along * along + coef_b * coef_b)
        vector = (along * vector + coef_b * unit_dir) / combined
        image = (along * image + coef_b * image_unit) / combined
        energy = lowest
    vector_share = lax.dynamic_slice_in_dim(vector, offset, owned, 0)
    return (vector_share[None], jnp.reshape(energy, (1,)))


def solution(mesh):
    placed = (
        P("chain", None, None, None),
        P("chain", None, None, None),
        P("chain", "term", None, None, None),
        P("chain", "term", None, None, None),
        P("chain", None, None),
    )
    return jax.shard_map(
        local,
        mesh=mesh,
        in_specs=placed,
        out_specs=(P("chain", "term", None, None), P("chain")),
        check_vma=False,
    )
```

profile of v0, /device:TPU:2, one launch (start us, length us, event | category | flops | bytes accessed | tf_op | source)
XLA Modules:
  0.0 458.2 jit_solution(8209784709253944239)
XLA Ops:
  7.2 5.4 %copy.8 = f32[1,8,8,128,128]{3,4,2,1,0:T(8,128)} copy(f32[1,8,8,128,128]{4,3,2,1,0:T(8,128)} %param.7) | data formatting | bytes 8388608 | tf_op args[2]
  14.6 3.6 collective-permute-start.3
  18.6 3.9 collective-permute-start.2
  26.0 36.8 %collective-permute-done.1 = f32[8,8,128,128]{2,3,1,0:T(8,128)} collective-permute-done((f32[8,8,128,128]{2,3,1,0:T(8,128)}, f32[8,8,128,128]{2,3,1,0:T(8,128)}, u32[]{:S(2)}, u32[]{:S(2)}) %collective-permute-start.1) | collective-permute-done | bytes 4194336 | tf_op jit(solution)/shard_map/ppermute | solution.py:17
  62.8 6.5 %broadcast_select_fusion.1 = f32[8,8,128,128]{2,3,1,0:T(8,128)} fusion(f32[8,8,128,128]{2,3,1,0:T(8,128)} %collective-permute-done.1, pred[]{:T(512)S(6)} %eq.18, f32[1,8,8,128,128]{3,4,2,1,0:T(8,128)} %copy.8), kind=kLoop, calls=%fused_computation.38 | loop fusion | flops 1048576 | bytes 12582913 | tf_op jit(solution)/shard_map/jit(_where)/select_n | solution.py:53
  69.3 5.5 %copy.9 = f32[8,8,128,128]{3,2,1,0:T(8,128)} copy(f32[8,8,128,128]{2,3,1,0:T(8,128)} %broadcast_select_fusion.1) | data formatting | bytes 8388608 | tf_op jit(solution)/shard_map/jit(_where)/select_n | solution.py:53
  74.8 6.7 %broadcast_select_fusion = f32[8,8,128,128]{3,2,1,0:T(8,128)} fusion(f32[8,8,128,128]{3,2,1,0:T(8,128)} %collective-permute-done.3, pred[]{:T(512)S(6)} %eq.20, f32[1,8,8,128,128]{4,3,2,1,0:T(8,128)} %param.8), kind=kLoop, calls=%fused_computation.37 | loop fusion | flops 1048576 | bytes 12582913 | tf_op jit(solution)/shard_map/jit(_where)/select_n | solution.py:54
  81.5 4.2 fusion.33
  85.7 5.1 %fusion.28 = f32[8,8,128,128]{3,2,1,0:T(8,128)} fusion(f32[8,128,8,128]{3,1,2,0:T(8,128)S(1)} %fusion.33, f32[8,128,128]{2,1,0:T(8,128)S(1)} %collective-permute-done, f32[128,128]{1,0:T(8,128)S(1)} %fusion.90, pred[]{:T(512)S(6)} %eq.18), kind=kOutput, calls=%fused_computation.29 | convolution fusion | flops 1610743808 | bytes 8978433 | tf_op jit(solution)/shard_map/kji,tkjm->tkim/dot_general | solution.py:61
  90.8 5.3 %copy.10 = f32[8,8,128,128]{2,3,1,0:T(8,128)} copy(f32[8,8,128,128]{3,2,1,0:T(8,128)} %broadcast_select_fusion) | data formatting | bytes 8388608 | tf_op jit(solution)/shard_map/jit(_where)/select_n | solution.py:54
  96.1 9.0 %fusion.26 = f32[8,128,8,128]{1,3,2,0:T(8,128)S(1)} fusion(f32[8,8,128,128]{3,2,1,0:T(8,128)} %fusion.28, f32[1,8,128,128]{3,2,1,0:T(8,128)S(1)} %copy-done.7, f32[]{:T(128)S(6)} %sqrt.39, f32[8,128]{1,0:T(8,128)S(1)} %get-tuple-element.21, f32[8,128]{1,0:T(8,128)S(1)} %get-tuple-element.20), kind=kOutput, calls=%fused_computation.27 | convolution fusion | flops 1611005952 | bytes 8921092 | tf_op jit(solution)/shard_map/tkij,kjl->tkil/dot_general | solution.py:66
  105.2 4.4 fusion.31
  109.6 4.3 fusion.14
  113.9 2.0 copy-done
  115.9 5.3 %fusion.35 = f32[8,128,128]{2,1,0:T(8,128)} fusion(f32[8,128,8,128]{3,1,2,0:T(8,128)S(1)} %fusion.14, f32[8,128,8,128]{1,3,2,0:T(8,128)S(1)} %fusion.26), kind=kOutput, calls=%fused_computation.45 | convolution fusion | flops 1610612736 | bytes 8912896 | tf_op jit(solution)/shard_map/tkil,tklm->kim/dot_general | solution.py:67
  121.2 52.0 %all-reduce.6.cloned.1.call-done = f32[8,128,128]{2,1,0:T(8,128)} async-done(((f32[8,128,128]{2,1,0:T(8,128)}), f32[8,128,128]{2,1,0:T(8,128)}) %all-reduce.6.cloned.1.call-update) | async-done | bytes 524304 | tf_op jit(solution)/shard_map/psum | solution.py:77
  178.3 8.9 %fusion.24 = f32[8,128,8,128]{1,3,2,0:T(8,128)S(1)} fusion(f32[8,8,128,128]{3,2,1,0:T(8,128)} %fusion.28, f32[]{:T(128)S(6)} %sqrt.40, f32[]{:T(128)S(6)} %div.131, f32[8,128,128]{2,1,0:T(8,128)} %all-reduce.6.cloned.1.call-done, f32[8,128]{1,0:T(8,128)S(1)} %get-tuple-element.21, f32[8,128]{1,0:T(8,128)S(1)} %get-tuple-element.20, ...), kind=kOutput, calls=%fused_computation.25 | convolution fusion | flops 1611530240 | bytes 9445388 | tf_op jit(solution)/shard_map/tkij,kjl->tkil/dot_general | solution.py:66
  187.3 4.8 %fusion.40 = f32[8,128,128]{2,1,0:T(8,128)} fusion(f32[8,128,8,128]{3,1,2,0:T(8,128)S(1)} %copy-done.1, f32[8,128,8,128]{1,3,2,0:T(8,128)S(1)} %fusion.24), kind=kOutput, calls=%fused_computation.46 | convolution fusion | flops 1610612736 | bytes 8912896 | tf_op jit(solution)/shard_map/tkil,tklm->kim/dot_general | solution.py:67
  192.1 48.8 %all-reduce.8.cloned.1.call-done = f32[8,128,128]{2,1,0:T(8,128)} async-done(((f32[8,128,128]{2,1,0:T(8,128)}), f32[8,128,128]{2,1,0:T(8,128)}) %all-reduce.8.cloned.1.call-update) | async-done | bytes 524304 | tf_op jit(solution)/shard_map/psum | solution.py:77
  240.9 1.9 multiply_reduce_fusion.8
  244.3 2.1 multiply_reduce_fusion.6
  247.1 8.8 %fusion.22 = f32[8,128,8,128]{1,3,2,0:T(8,128)S(1)} fusion(f32[8,8,128,128]{3,2,1,0:T(8,128)} %fusion.28, f32[]{:T(128)S(6)} %sqrt.43, f32[8,128,128]{2,1,0:T(8,128)S(1)} %get-tuple-element.17, f32[8,128,128]{2,1,0:T(8,128)S(1)} %get-tuple-element.16, f32[]{:T(128)S(6)} %sub.54), kind=kOutput, calls=%fused_computation.23 | convolution fusion | flops 1611005952 | bytes 9437192 | tf_op jit(solution)/shard_map/tkij,kjl->tkil/dot_general | solution.py:66
  255.9 4.8 %fusion.45 = f32[8,128,128]{2,1,0:T(8,128)} fusion(f32[8,128,8,128]{3,1,2,0:T(8,128)S(1)} %copy-done.2, f32[8,128,8,128]{1,3,2,0:T(8,128)S(1)} %fusion.22), kind=kOutput, calls=%fused_computation.47 | convolution fusion | flops 1610612736 | bytes 8912896 | tf_op jit(solution)/shard_map/tkil,tklm->kim/dot_general | solution.py:67
  260.8 48.8 %all-reduce.10.cloned.1.call-done = f32[8,128,128]{2,1,0:T(8,128)} async-done(((f32[8,128,128]{2,1,0:T(8,128)}), f32[8,128,128]{2,1,0:T(8,128)}) %all-reduce.10.cloned.1.call-update) | async-done | bytes 524304 | tf_op jit(solution)/shard_map/psum | solution.py:77
  313.0 2.0 multiply_reduce_fusion.3
  315.6 8.9 %fusion.20 = f32[8,128,8,128]{1,3,2,0:T(8,128)S(1)} fusion(f32[8,8,128,128]{3,2,1,0:T(8,128)} %fusion.28, f32[]{:T(128)S(6)} %sqrt.46, f32[8,128,128]{2,1,0:T(8,128)S(1)} %get-tuple-element.14, f32[8,128,128]{2,1,0:T(8,128)S(1)} %get-tuple-element.13, f32[]{:T(128)S(6)} %sub.58), kind=kOutput, calls=%fused_computation.21 | convolution fusion | flops 1611005952 | bytes 9437192 | tf_op jit(solution)/shard_map/tkij,kjl->tkil/dot_general | solution.py:66
  324.5 4.8 %fusion.50 = f32[8,128,128]{2,1,0:T(8,128)} fusion(f32[8,128,8,128]{3,1,2,0:T(8,128)S(1)} %copy-done.3, f32[8,128,8,128]{1,3,2,0:T(8,128)S(1)} %fusion.20), kind=kOutput, calls=%fused_computation.48 | convolution fusion | flops 1610612736 | bytes 8912896 | tf_op jit(solution)/shard_map/tkil,tklm->kim/dot_general | solution.py:67
  329.4 48.8 %all-reduce.12.cloned.1.call-done = f32[8,128,128]{2,1,0:T(8,128)} async-done(((f32[8,128,128]{2,1,0:T(8,128)}), f32[8,128,128]{2,1,0:T(8,128)}) %all-reduce.12.cloned.1.call-update) | async-done | bytes 524304 | tf_op jit(solution)/shard_map/psum | solution.py:77
  381.6 2.0 multiply_reduce_fusion.1
  384.3 8.9 %fusion.18 = f32[8,128,8,128]{1,3,2,0:T(8,128)S(1)} fusion(f32[8,8,128,128]{3,2,1,0:T(8,128)} %fusion.28, f32[8,128,128]{2,1,0:T(8,128)S(1)} %broadcast_divide_fusion), kind=kOutput, calls=%fused_computation.19 | convolution fusion | flops 1610612736 | bytes 8912896 | tf_op jit(solution)/shard_map/tkij,kjl->tkil/dot_general | solution.py:66
  393.2 4.8 %fusion.55 = f32[8,128,128]{2,1,0:T(8,128)} fusion(f32[8,128,8,128]{3,1,2,0:T(8,128)S(1)} %copy-done.4, f32[8,128,8,128]{1,3,2,0:T(8,128)S(1)} %fusion.18), kind=kOutput, calls=%fused_computation.49 | convolution fusion | flops 1610612736 | bytes 8912896 | tf_op jit(solution)/shard_map/tkil,tklm->kim/dot_general | solution.py:67
  398.7 48.2 %all-reduce.14.cloned.1.call-done = f32[8,128,128]{2,1,0:T(8,128)} async-done(((f32[8,128,128]{2,1,0:T(8,128)}), f32[8,128,128]{2,1,0:T(8,128)}) %all-reduce.14.cloned.1.call-update) | async-done | bytes 524304 | tf_op jit(solution)/shard_map/psum | solution.py:77
  (53 shorter events, 15.4 us)
Async XLA Ops:
  7.2 11.1 %copy-start.11 = (f32[1,8,128,128]{3,2,1,0:T(8,128)S(1)}, f32[1,8,128,128]{3,2,1,0:T(8,128)}, u32[]{:S(2)}) copy-start(f32[1,8,128,128]{3,2,1,0:T(8,128)} %param.6) | copy-start | bytes 1572868
  7.2 17.2 %copy-start.12 = (s32[1,2,8]{2,1,0:T(2,128)S(1)}, s32[1,2,8]{2,1,0:T(2,128)}, u32[]{:S(2)}) copy-start(s32[1,2,8]{2,1,0:T(2,128)} %param.9) | copy-start | bytes 196
  7.2 17.3 %copy-start.7 = (f32[1,8,128,128]{3,2,1,0:T(8,128)S(1)}, f32[1,8,128,128]{3,2,1,0:T(8,128)}, u32[]{:S(2)}) copy-start(f32[1,8,128,128]{3,2,1,0:T(8,128)} %param.5) | copy-start | bytes 1572868
  7.2 166.1 %all-reduce.6.cloned.1.call-start = ((), (), s32[]{:S(2)}) async-start(), calls=%async_computation | async-start | bytes 1048576 | tf_op jit(solution)/shard_map/psum | solution.py:77
  12.7 50.1 %collective-permute-start.1 = (f32[8,8,128,128]{2,3,1,0:T(8,128)}, f32[8,8,128,128]{2,3,1,0:T(8,128)}, u32[]{:S(2)}, u32[]{:S(2)}) collective-permute-start(f32[8,8,128,128]{2,3,1,0:T(8,128)} %bitcast.173), channel_id=1, source_target_pairs={{0,4},{4,8},{8,12},{12,16},{16,20},{20,24},{24,28},{28,32},{32,36}... | collective-permute-start | bytes 12582920 | tf_op jit(solution)/shard_map/ppermute | solution.py:17
  14.6 60.2 %collective-permute-start.3 = (f32[8,8,128,128]{3,2,1,0:T(8,128)}, f32[8,8,128,128]{3,2,1,0:T(8,128)}, u32[]{:S(2)}, u32[]{:S(2)}) collective-permute-start(f32[8,8,128,128]{3,2,1,0:T(8,128)} %bitcast.174), channel_id=1, source_target_pairs={{4,0},{8,4},{12,8},{16,12},{20,16},{24,20},{28,24},{32,28},{36,32}... | collective-permute-start | bytes 12582920 | tf_op jit(solution)/shard_map/ppermute | solution.py:17
  18.6 86.6 %collective-permute-start.2 = (f32[8,128,128]{2,1,0:T(8,128)S(1)}, f32[8,128,128]{2,1,0:T(8,128)S(1)}, u32[]{:S(2)}, u32[]{:S(2)}) collective-permute-start(f32[8,128,128]{2,1,0:T(8,128)S(1)} %fusion.73), channel_id=1, source_target_pairs={{4,0},{8,4},{12,8},{16,12},{20,16},{24,20},{28,24},{32,28},{36,32}... | collective-permute-start | bytes 1572872 | tf_op jit(solution)/shard_map/ppermute | solution.py:17
  22.5 59.0 %collective-permute-start = (f32[8,128,128]{2,1,0:T(8,128)S(1)}, f32[8,128,128]{2,1,0:T(8,128)S(1)}, u32[]{:S(2)}, u32[]{:S(2)}) collective-permute-start(f32[8,128,128]{2,1,0:T(8,128)S(1)} %fusion.73), channel_id=1, source_target_pairs={{0,4},{4,8},{8,12},{12,16},{16,20},{20,24},{24,28},{28,32},{32,36}... | collective-permute-start | bytes 1572872 | tf_op jit(solution)/shard_map/ppermute | solution.py:17
  74.8 6.7 %copy-start.6 = (f32[8,8,128,128]{2,3,1,0:T(8,128)S(1)}, f32[8,8,128,128]{2,3,1,0:T(8,128)}, u32[]{:S(2)}) copy-start(f32[8,8,128,128]{2,3,1,0:T(8,128)} %broadcast_select_fusion.1) | copy-start | bytes 12582916
  74.8 6.7 %copy-start.8 = (f32[8,8,128,128]{3,2,1,0:T(8,128)S(1)}, f32[8,8,128,128]{3,2,1,0:T(8,128)}, u32[]{:S(2)}) copy-start(f32[8,8,128,128]{3,2,1,0:T(8,128)} %copy.9) | copy-start | bytes 12582916
  96.1 9.1 %copy-start.5 = (f32[8,8,128,128]{3,2,1,0:T(8,128)S(1)}, f32[8,8,128,128]{3,2,1,0:T(8,128)}, u32[]{:S(2)}) copy-start(f32[8,8,128,128]{3,2,1,0:T(8,128)} %broadcast_select_fusion) | copy-start | bytes 12582916
  96.1 9.1 %copy-start.9 = (f32[8,8,128,128]{2,3,1,0:T(8,128)S(1)}, f32[8,8,128,128]{2,3,1,0:T(8,128)}, u32[]{:S(2)}) copy-start(f32[8,8,128,128]{2,3,1,0:T(8,128)} %copy.10) | copy-start | bytes 12582916
  113.9 2.0 copy-start
  121.2 119.8 %all-reduce.8.cloned.1.call-start = ((), (), s32[]{:S(2)}) async-start(), calls=%async_computation.1 | async-start | bytes 1048576 | tf_op jit(solution)/shard_map/psum | solution.py:77
  178.3 8.9 %copy-start.1 = (f32[8,128,8,128]{3,1,2,0:T(8,128)S(1)}, f32[8,128,8,128]{3,1,2,0:T(8,128)}, u32[]{:S(2)}) copy-start(f32[8,128,8,128]{3,1,2,0:T(8,128)} %copy-done) | copy-start | bytes 12582916
  187.3 53.7 %copy-start.10 = (f32[8,128,128]{2,1,0:T(8,128)S(1)}, f32[8,128,128]{2,1,0:T(8,128)}, u32[]{:S(2)}) copy-start(f32[8,128,128]{2,1,0:T(8,128)} %all-reduce.6.cloned.1.call-done) | copy-start | bytes 1572868
  192.1 117.6 %all-reduce.10.cloned.1.call-start = ((), (), s32[]{:S(2)}) async-start(), calls=%async_computation.2 | async-start | bytes 1048576 | tf_op jit(solution)/shard_map/psum | solution.py:77
  247.1 8.8 %copy-start.2 = (f32[8,128,8,128]{3,1,2,0:T(8,128)S(1)}, f32[8,128,8,128]{3,1,2,0:T(8,128)}, u32[]{:S(2)}) copy-start(f32[8,128,8,128]{3,1,2,0:T(8,128)} %copy-done) | copy-start | bytes 12582916
  260.8 117.5 %all-reduce.12.cloned.1.call-start = ((), (), s32[]{:S(2)}) async-start(), calls=%async_computation.3 | async-start | bytes 1048576 | tf_op jit(solution)/shard_map/psum | solution.py:77
  315.6 8.9 %copy-start.3 = (f32[8,128,8,128]{3,1,2,0:T(8,128)S(1)}, f32[8,128,8,128]{3,1,2,0:T(8,128)}, u32[]{:S(2)}) copy-start(f32[8,128,8,128]{3,1,2,0:T(8,128)} %copy-done) | copy-start | bytes 12582916
  329.4 117.6 %all-reduce.14.cloned.1.call-start = ((), (), s32[]{:S(2)}) async-start(), calls=%async_computation.4 | async-start | bytes 1048576 | tf_op jit(solution)/shard_map/psum | solution.py:77
  384.3 8.9 %copy-start.4 = (f32[8,128,8,128]{3,1,2,0:T(8,128)S(1)}, f32[8,128,8,128]{3,1,2,0:T(8,128)}, u32[]{:S(2)}) copy-start(f32[8,128,8,128]{3,1,2,0:T(8,128)} %copy-done) | copy-start | bytes 12582916
Sparse Core Ops, SparseCore 0:
  121.3 51.9 all-reduce.5
  192.2 48.7 all-reduce.7
  260.9 48.7 all-reduce.9
  329.5 48.7 all-reduce.11
  398.2 48.7 all-reduce.13
where the time goes:
time: 461 us; the launch traced here: 458 us
  waiting for transfers between devices  284 us (62%)
  matrix products  86.9 us (19%)
  other arithmetic  32.2 us (7%)
  between operations  25.4 us (6%)
  local copies, waits for them, and re-layouts  18.5 us (4%)
  starting transfers between devices  11.6 us (3%)
    psum x5, waiting for transfers between devices, apply_whole(): return finish(lax.psum(partial_term(direction), 'term'))  247 us
    dot_general x5, matrix products, partial_term(): halfway = jnp.einsum('tkij,kjl->tkil', left_full, vector, precision=precise)  44.5 us
    ppermute x4, waiting for transfers between devices, from_behind(): lax.ppermute(value, axis, [(source, source + steps) for source in range(l...  36.8 us
    dot_general x5, matrix products, partial_term(): return jnp.einsum('tkil,tklm->kim', halfway, right_full, precision=precise)  24.4 us
    reduce_sum x9, other arithmetic, mean_dot(): return jnp.sum(first_arr * second_arr) / volume  17.2 us
    ppermute x4, starting transfers between devices, from_behind(): lax.ppermute(value, axis, [(source, source + steps) for source in range(l...  11.4 us
  transfers between devices with their start and end apart: 9, of which 6 were waited for; matrix products, arithmetic and copies ran while one was open for 9% of the time, Pallas kernels for 0%

commit v1 on v0

--- a/solution.py
+++ b/solution.py
@@ -74,7 +74,7 @@
     vector = started / start_norm
 
     def apply_whole(direction):
-        return finish(lax.psum(partial_term(direction), "term"))
+        return finish(lax.all_gather(partial_term(direction), axis_name="term").sum(axis=0))
 
     def mean_dot(first_arr, second_arr):
         return jnp.sum(first_arr * second_arr) / volume

time: 461 us -> 385 us (0.84)
  waiting for transfers between devices: 284 us -> 208 us
    psum x5 -> x0, waiting for transfers between devices: 247 us -> none  [apply_whole(): return finish(lax.psum(partial_term(direction), 'term'))]
    all_gather x0 -> x5, waiting for transfers between devices: none -> 171 us  [apply_whole(): lax.all_gather(partial_term(direction), axis_name='term').sum(axis=0)]
    reduce_sum x9, other arithmetic: 17.2 us -> 7.84 us  [mean_dot(): return jnp.sum(first_arr * second_arr) / volume]
    reduce_sum x0 -> x5, other arithmetic: none -> 8.8 us  [apply_whole(): lax.all_gather(partial_term(direction), axis_name='term').sum(axis=0)]
  transfers between devices with their start and end apart: 9 -> 9, of which waited for: 6 -> 6; matrix products, arithmetic and copies ran while one was open for 9% -> 11% of each run, Pallas kernels for 0% -> 0%
where the time goes in v1:
time: 385 us; the launch traced here: 381 us
  waiting for transfers between devices  208 us (54%)
  matrix products  86.7 us (23%)
  other arithmetic  31.6 us (8%)
  between operations  25.4 us (7%)
  local copies, waits for them, and re-layouts  18.5 us (5%)
  starting transfers between devices  11.6 us (3%)
    all_gather x5, waiting for transfers between devices, apply_whole(): lax.all_gather(partial_term(direction), axis_name='term').sum(axis=0)  171 us
    dot_general x5, matrix products, partial_term(): halfway = jnp.einsum('tkij,kjl->tkil', left_full, vector, precision=precise)  44.4 us
    ppermute x4, waiting for transfers between devices, from_behind(): lax.ppermute(value, axis, [(source, source + steps) for source in range(l...  36.8 us
    dot_general x5, matrix products, partial_term(): return jnp.einsum('tkil,tklm->kim', halfway, right_full, precision=precise)  24.3 us
    ppermute x4, starting transfers between devices, from_behind(): lax.ppermute(value, axis, [(source, source + steps) for source in range(l...  11.4 us
    reduce_sum x5, other arithmetic, apply_whole(): lax.all_gather(partial_term(direction), axis_name='term').sum(axis=0)  8.8 us
    reduce_sum x9, other arithmetic, mean_dot(): return jnp.sum(first_arr * second_arr) / volume  7.84 us
  transfers between devices with their start and end apart: 9, of which 6 were waited for; matrix products, arithmetic and copies ran while one was open for 11% of the time, Pallas kernels for 0%

profile of v1, /device:TPU:2, one launch (start us, length us, event | category | flops | bytes accessed | tf_op | source)
XLA Modules:
  0.0 381.5 jit_solution(1138106757067383491)
XLA Ops:
  7.2 5.4 %copy.17 = f32[1,8,8,128,128]{3,4,2,1,0:T(8,128)} copy(f32[1,8,8,128,128]{4,3,2,1,0:T(8,128)} %param.7) | data formatting | bytes 8388608 | tf_op args[2]
  12.7 1.9 collective-permute-start.1
  14.6 3.6 collective-permute-start.3
  18.6 3.9 %collective-permute-start.2 = (f32[8,128,128]{2,1,0:T(8,128)S(1)}, f32[8,128,128]{2,1,0:T(8,128)S(1)}, u32[]{:S(2)}, u32[]{:S(2)}) collective-permute-start(f32[8,128,128]{2,1,0:T(8,128)S(1)} %fusion.73), channel_id=1, source_target_pairs={{4,0},{8,4},{12,8},{16,12},{20,16},{24,20},{28,24},{32,28},{36,32}... | collective-permute-start | bytes 1572872 | tf_op jit(solution)/shard_map/ppermute | solution.py:17
  22.5 1.9 collective-permute-start
  26.0 36.8 %collective-permute-done.1 = f32[8,8,128,128]{2,3,1,0:T(8,128)} collective-permute-done((f32[8,8,128,128]{2,3,1,0:T(8,128)}, f32[8,8,128,128]{2,3,1,0:T(8,128)}, u32[]{:S(2)}, u32[]{:S(2)}) %collective-permute-start.1) | collective-permute-done | bytes 4194336 | tf_op jit(solution)/shard_map/ppermute | solution.py:17
  62.8 6.5 %broadcast_select_fusion.1 = f32[8,8,128,128]{2,3,1,0:T(8,128)} fusion(f32[8,8,128,128]{2,3,1,0:T(8,128)} %collective-permute-done.1, pred[]{:T(512)S(6)} %eq.18, f32[1,8,8,128,128]{3,4,2,1,0:T(8,128)} %copy.17), kind=kLoop, calls=%fused_computation.38 | loop fusion | flops 1048576 | bytes 12582913 | tf_op jit(solution)/shard_map/jit(_where)/select_n | solution.py:53
  69.3 5.5 %copy.18 = f32[8,8,128,128]{3,2,1,0:T(8,128)} copy(f32[8,8,128,128]{2,3,1,0:T(8,128)} %broadcast_select_fusion.1) | data formatting | bytes 8388608 | tf_op jit(solution)/shard_map/jit(_where)/select_n | solution.py:53
  74.8 6.7 %broadcast_select_fusion = f32[8,8,128,128]{3,2,1,0:T(8,128)} fusion(f32[8,8,128,128]{3,2,1,0:T(8,128)} %collective-permute-done.3, pred[]{:T(512)S(6)} %eq.20, f32[1,8,8,128,128]{4,3,2,1,0:T(8,128)} %param.8), kind=kLoop, calls=%fused_computation.37 | loop fusion | flops 1048576 | bytes 12582913 | tf_op jit(solution)/shard_map/jit(_where)/select_n | solution.py:54
  81.5 4.2 %fusion.33 = f32[8,128,8,128]{3,1,2,0:T(8,128)S(1)} fusion(f32[8,128,128]{2,1,0:T(8,128)S(1)} %collective-permute-done, f32[128,128]{1,0:T(8,128)S(1)} %fusion.90, pred[]{:T(512)S(6)} %eq.18, f32[8,8,128,128]{3,2,1,0:T(8,128)S(1)} %copy-done.8, f32[8,8,128,128]{2,3,1,0:T(8,128)S(1)} %copy-done.6), kind=kOutput, calls=%fused_computation.35 | convolution fusion | flops 1612840960 | bytes 13172737 | tf_op jit(solution)/shard_map/tkjl,klm->tkjm/dot_general | solution.py:60
  85.7 5.1 %fusion.28 = f32[8,8,128,128]{3,2,1,0:T(8,128)} fusion(f32[8,128,8,128]{3,1,2,0:T(8,128)S(1)} %fusion.33, f32[8,128,128]{2,1,0:T(8,128)S(1)} %collective-permute-done, f32[128,128]{1,0:T(8,128)S(1)} %fusion.90, pred[]{:T(512)S(6)} %eq.18), kind=kOutput, calls=%fused_computation.29 | convolution fusion | flops 1610743808 | bytes 8978433 | tf_op jit(solution)/shard_map/kji,tkjm->tkim/dot_general | solution.py:61
  90.8 5.3 %copy.19 = f32[8,8,128,128]{2,3,1,0:T(8,128)} copy(f32[8,8,128,128]{3,2,1,0:T(8,128)} %broadcast_select_fusion) | data formatting | bytes 8388608 | tf_op jit(solution)/shard_map/jit(_where)/select_n | solution.py:54
  96.1 9.0 %fusion.26 = f32[8,128,8,128]{1,3,2,0:T(8,128)S(1)} fusion(f32[8,8,128,128]{3,2,1,0:T(8,128)} %fusion.28, f32[1,8,128,128]{3,2,1,0:T(8,128)S(1)} %copy-done.7, f32[]{:T(128)S(6)} %sqrt.39, f32[8,128]{1,0:T(8,128)S(1)} %get-tuple-element.21, f32[8,128]{1,0:T(8,128)S(1)} %get-tuple-element.20), kind=kOutput, calls=%fused_computation.27 | convolution fusion | flops 1611005952 | bytes 8921092 | tf_op jit(solution)/shard_map/tkij,kjl->tkil/dot_general | solution.py:66
  105.2 4.4 %fusion.31 = f32[8,8,128,128]{2,3,1,0:T(8,128)S(1)} fusion(f32[8,128,128]{2,1,0:T(8,128)S(1)} %collective-permute-done.2, f32[128,128]{1,0:T(8,128)S(1)} %fusion.90, pred[]{:T(512)S(6)} %eq.20, f32[8,8,128,128]{3,2,1,0:T(8,128)S(1)} %copy-done.5, f32[8,8,128,128]{2,3,1,0:T(8,128)S(1)} %copy-done.9), kind=kOutput, calls=%fused_computation.33 | convolution fusion | flops 1612840960 | bytes 13172737 | tf_op jit(solution)/shard_map/kij,tkjl->tkil/dot_general | solution.py:62
  109.6 4.3 %fusion.14 = f32[8,128,8,128]{3,1,2,0:T(8,128)S(1)} fusion(f32[8,8,128,128]{2,3,1,0:T(8,128)S(1)} %fusion.31, f32[8,128,128]{2,1,0:T(8,128)S(1)} %collective-permute-done.2, f32[128,128]{1,0:T(8,128)S(1)} %fusion.90, pred[]{:T(512)S(6)} %eq.20), kind=kOutput, calls=%fused_computation.14 | convolution fusion | flops 1610743808 | bytes 8978433 | tf_op jit(solution)/shard_map/tkil,kml->tkim/dot_general | solution.py:63
  113.9 2.0 copy-done
  115.9 5.2 %fusion.35 = f32[8,128,128]{2,1,0:T(8,128)} fusion(f32[8,128,8,128]{3,1,2,0:T(8,128)S(1)} %fusion.14, f32[8,128,8,128]{1,3,2,0:T(8,128)S(1)} %fusion.26), kind=kOutput, calls=%fused_computation.45 | convolution fusion | flops 1610612736 | bytes 8912896 | tf_op jit(solution)/shard_map/tkil,tklm->kim/dot_general | solution.py:67
  121.2 37.3 %all-gather.11.cloned.1.call-done = f32[32,128,128]{2,1,0:T(8,128)} async-done(((f32[8,128,128]{2,1,0:T(8,128)}), f32[32,128,128]{2,1,0:T(8,128)}) %all-gather.11.cloned.1.call-update) | async-done | bytes 2097168 | tf_op jit(solution)/shard_map/all_gather | solution.py:77
  163.2 8.8 %fusion.24 = f32[8,128,8,128]{1,3,2,0:T(8,128)S(1)} fusion(f32[8,8,128,128]{3,2,1,0:T(8,128)} %fusion.28, f32[]{:T(128)S(6)} %sqrt.40, f32[]{:T(128)S(6)} %div.131, f32[8,128,128]{2,1,0:T(8,128)S(1)} %reduce_sum.172, f32[8,128]{1,0:T(8,128)S(1)} %get-tuple-element.21, f32[8,128]{1,0:T(8,128)S(1)} %get-tuple-element.20, ...), kind=kOutput, calls=%fused_computation.25 | convolution fusion | flops 1611530240 | bytes 9445388 | tf_op jit(solution)/shard_map/tkij,kjl->tkil/dot_general | solution.py:66
  172.1 4.8 %fusion.40 = f32[8,128,128]{2,1,0:T(8,128)} fusion(f32[8,128,8,128]{3,1,2,0:T(8,128)S(1)} %copy-done.1, f32[8,128,8,128]{1,3,2,0:T(8,128)S(1)} %fusion.24), kind=kOutput, calls=%fused_computation.46 | convolution fusion | flops 1610612736 | bytes 8912896 | tf_op jit(solution)/shard_map/tkil,tklm->kim/dot_general | solution.py:67
  176.9 33.6 %all-gather.13.cloned.1.call-done = f32[32,128,128]{2,1,0:T(8,128)} async-done(((f32[8,128,128]{2,1,0:T(8,128)}), f32[32,128,128]{2,1,0:T(8,128)}) %all-gather.13.cloned.1.call-update) | async-done | bytes 2097168 | tf_op jit(solution)/shard_map/all_gather | solution.py:77
  216.3 8.8 %fusion.22 = f32[8,128,8,128]{1,3,2,0:T(8,128)S(1)} fusion(f32[8,8,128,128]{3,2,1,0:T(8,128)} %fusion.28, f32[]{:T(128)S(6)} %sqrt.43, f32[8,128,128]{2,1,0:T(8,128)S(1)} %get-tuple-element.17, f32[8,128,128]{2,1,0:T(8,128)S(1)} %get-tuple-element.16, f32[]{:T(128)S(6)} %sub.54), kind=kOutput, calls=%fused_computation.23 | convolution fusion | flops 1611005952 | bytes 9437192 | tf_op jit(solution)/shard_map/tkij,kjl->tkil/dot_general | solution.py:66
  225.1 4.8 %fusion.45 = f32[8,128,128]{2,1,0:T(8,128)} fusion(f32[8,128,8,128]{3,1,2,0:T(8,128)S(1)} %copy-done.2, f32[8,128,8,128]{1,3,2,0:T(8,128)S(1)} %fusion.22), kind=kOutput, calls=%fused_computation.47 | convolution fusion | flops 1610612736 | bytes 8912896 | tf_op jit(solution)/shard_map/tkil,tklm->kim/dot_general | solution.py:67
  230.0 33.6 %all-gather.15.cloned.1.call-done = f32[32,128,128]{2,1,0:T(8,128)} async-done(((f32[8,128,128]{2,1,0:T(8,128)}), f32[32,128,128]{2,1,0:T(8,128)}) %all-gather.15.cloned.1.call-update) | async-done | bytes 2097168 | tf_op jit(solution)/shard_map/all_gather | solution.py:77
  263.6 1.8 reduce_sum.180
  269.2 8.9 %fusion.20 = f32[8,128,8,128]{1,3,2,0:T(8,128)S(1)} fusion(f32[8,8,128,128]{3,2,1,0:T(8,128)} %fusion.28, f32[]{:T(128)S(6)} %sqrt.46, f32[8,128,128]{2,1,0:T(8,128)S(1)} %get-tuple-element.14, f32[8,128,128]{2,1,0:T(8,128)S(1)} %get-tuple-element.13, f32[]{:T(128)S(6)} %sub.58), kind=kOutput, calls=%fused_computation.21 | convolution fusion | flops 1611005952 | bytes 9437192 | tf_op jit(solution)/shard_map/tkij,kjl->tkil/dot_general | solution.py:66
  278.1 4.8 %fusion.50 = f32[8,128,128]{2,1,0:T(8,128)} fusion(f32[8,128,8,128]{3,1,2,0:T(8,128)S(1)} %copy-done.3, f32[8,128,8,128]{1,3,2,0:T(8,128)S(1)} %fusion.20), kind=kOutput, calls=%fused_computation.48 | convolution fusion | flops 1610612736 | bytes 8912896 | tf_op jit(solution)/shard_map/tkil,tklm->kim/dot_general | solution.py:67
  282.9 33.5 %all-gather.17.cloned.1.call-done = f32[32,128,128]{2,1,0:T(8,128)} async-done(((f32[8,128,128]{2,1,0:T(8,128)}), f32[32,128,128]{2,1,0:T(8,128)}) %all-gather.17.cloned.1.call-update) | async-done | bytes 2097168 | tf_op jit(solution)/shard_map/all_gather | solution.py:77
  316.5 1.8 reduce_sum.184
  322.2 8.9 %fusion.18 = f32[8,128,8,128]{1,3,2,0:T(8,128)S(1)} fusion(f32[8,8,128,128]{3,2,1,0:T(8,128)} %fusion.28, f32[8,128,128]{2,1,0:T(8,128)S(1)} %broadcast_divide_fusion), kind=kOutput, calls=%fused_computation.19 | convolution fusion | flops 1610612736 | bytes 8912896 | tf_op jit(solution)/shard_map/tkij,kjl->tkil/dot_general | solution.py:66
  331.1 4.8 %fusion.55 = f32[8,128,128]{2,1,0:T(8,128)} fusion(f32[8,128,8,128]{3,1,2,0:T(8,128)S(1)} %copy-done.4, f32[8,128,8,128]{1,3,2,0:T(8,128)S(1)} %fusion.18), kind=kOutput, calls=%fused_computation.49 | convolution fusion | flops 1610612736 | bytes 8912896 | tf_op jit(solution)/shard_map/tkil,tklm->kim/dot_general | solution.py:67
  336.6 32.9 %all-gather.19.cloned.1.call-done = f32[32,128,128]{2,1,0:T(8,128)} async-done(((f32[8,128,128]{2,1,0:T(8,128)}), f32[32,128,128]{2,1,0:T(8,128)}) %all-gather.19.cloned.1.call-update) | async-done | bytes 2097168 | tf_op jit(solution)/shard_map/all_gather | solution.py:77
  (56 shorter events, 15.4 us)
Async XLA Ops:
  7.2 11.1 %copy-start.10 = (f32[1,8,128,128]{3,2,1,0:T(8,128)S(1)}, f32[1,8,128,128]{3,2,1,0:T(8,128)}, u32[]{:S(2)}) copy-start(f32[1,8,128,128]{3,2,1,0:T(8,128)} %param.6) | copy-start | bytes 1572868
  7.2 17.2 %copy-start.11 = (s32[1,2,8]{2,1,0:T(2,128)S(1)}, s32[1,2,8]{2,1,0:T(2,128)}, u32[]{:S(2)}) copy-start(s32[1,2,8]{2,1,0:T(2,128)} %param.9) | copy-start | bytes 196
  7.2 17.3 %copy-start.7 = (f32[1,8,128,128]{3,2,1,0:T(8,128)S(1)}, f32[1,8,128,128]{3,2,1,0:T(8,128)}, u32[]{:S(2)}) copy-start(f32[1,8,128,128]{3,2,1,0:T(8,128)} %param.5) | copy-start | bytes 1572868
  7.2 151.3 %all-gather.11.cloned.1.call-start = ((), (), s32[]{:S(2)}) async-start(), calls=%async_computation | async-start | bytes 2621440 | tf_op jit(solution)/shard_map/all_gather | solution.py:77
  12.7 50.1 %collective-permute-start.1 = (f32[8,8,128,128]{2,3,1,0:T(8,128)}, f32[8,8,128,128]{2,3,1,0:T(8,128)}, u32[]{:S(2)}, u32[]{:S(2)}) collective-permute-start(f32[8,8,128,128]{2,3,1,0:T(8,128)} %bitcast.178), channel_id=1, source_target_pairs={{0,4},{4,8},{8,12},{12,16},{16,20},{20,24},{24,28},{28,32},{32,36}... | collective-permute-start | bytes 12582920 | tf_op jit(solution)/shard_map/ppermute | solution.py:17
  14.6 60.2 %collective-permute-start.3 = (f32[8,8,128,128]{3,2,1,0:T(8,128)}, f32[8,8,128,128]{3,2,1,0:T(8,128)}, u32[]{:S(2)}, u32[]{:S(2)}) collective-permute-start(f32[8,8,128,128]{3,2,1,0:T(8,128)} %bitcast.179), channel_id=1, source_target_pairs={{4,0},{8,4},{12,8},{16,12},{20,16},{24,20},{28,24},{32,28},{36,32}... | collective-permute-start | bytes 12582920 | tf_op jit(solution)/shard_map/ppermute | solution.py:17
  18.6 86.6 %collective-permute-start.2 = (f32[8,128,128]{2,1,0:T(8,128)S(1)}, f32[8,128,128]{2,1,0:T(8,128)S(1)}, u32[]{:S(2)}, u32[]{:S(2)}) collective-permute-start(f32[8,128,128]{2,1,0:T(8,128)S(1)} %fusion.73), channel_id=1, source_target_pairs={{4,0},{8,4},{12,8},{16,12},{20,16},{24,20},{28,24},{32,28},{36,32}... | collective-permute-start | bytes 1572872 | tf_op jit(solution)/shard_map/ppermute | solution.py:17
  22.5 59.0 %collective-permute-start = (f32[8,128,128]{2,1,0:T(8,128)S(1)}, f32[8,128,128]{2,1,0:T(8,128)S(1)}, u32[]{:S(2)}, u32[]{:S(2)}) collective-permute-start(f32[8,128,128]{2,1,0:T(8,128)S(1)} %fusion.73), channel_id=1, source_target_pairs={{0,4},{4,8},{8,12},{12,16},{16,20},{20,24},{24,28},{28,32},{32,36}... | collective-permute-start | bytes 1572872 | tf_op jit(solution)/shard_map/ppermute | solution.py:17
  74.8 6.7 %copy-start.6 = (f32[8,8,128,128]{2,3,1,0:T(8,128)S(1)}, f32[8,8,128,128]{2,3,1,0:T(8,128)}, u32[]{:S(2)}) copy-start(f32[8,8,128,128]{2,3,1,0:T(8,128)} %broadcast_select_fusion.1) | copy-start | bytes 12582916
  74.8 6.7 %copy-start.8 = (f32[8,8,128,128]{3,2,1,0:T(8,128)S(1)}, f32[8,8,128,128]{3,2,1,0:T(8,128)}, u32[]{:S(2)}) copy-start(f32[8,8,128,128]{3,2,1,0:T(8,128)} %copy.18) | copy-start | bytes 12582916
  96.1 9.1 %copy-start.5 = (f32[8,8,128,128]{3,2,1,0:T(8,128)S(1)}, f32[8,8,128,128]{3,2,1,0:T(8,128)}, u32[]{:S(2)}) copy-start(f32[8,8,128,128]{3,2,1,0:T(8,128)} %broadcast_select_fusion) | copy-start | bytes 12582916
  96.1 9.1 %copy-start.9 = (f32[8,8,128,128]{2,3,1,0:T(8,128)S(1)}, f32[8,8,128,128]{2,3,1,0:T(8,128)}, u32[]{:S(2)}) copy-start(f32[8,8,128,128]{2,3,1,0:T(8,128)} %copy.19) | copy-start | bytes 12582916
  113.9 2.0 copy-start
  121.1 89.4 %all-gather.13.cloned.1.call-start = ((), (), s32[]{:S(2)}) async-start(), calls=%async_computation.1 | async-start | bytes 2621440 | tf_op jit(solution)/shard_map/all_gather | solution.py:77
  163.2 8.8 %copy-start.1 = (f32[8,128,8,128]{3,1,2,0:T(8,128)S(1)}, f32[8,128,8,128]{3,1,2,0:T(8,128)}, u32[]{:S(2)}) copy-start(f32[8,128,8,128]{3,1,2,0:T(8,128)} %copy-done) | copy-start | bytes 12582916
  176.9 86.7 %all-gather.15.cloned.1.call-start = ((), (), s32[]{:S(2)}) async-start(), calls=%async_computation.2 | async-start | bytes 2621440 | tf_op jit(solution)/shard_map/all_gather | solution.py:77
  216.3 8.8 %copy-start.2 = (f32[8,128,8,128]{3,1,2,0:T(8,128)S(1)}, f32[8,128,8,128]{3,1,2,0:T(8,128)}, u32[]{:S(2)}) copy-start(f32[8,128,8,128]{3,1,2,0:T(8,128)} %copy-done) | copy-start | bytes 12582916
  230.0 86.5 %all-gather.17.cloned.1.call-start = ((), (), s32[]{:S(2)}) async-start(), calls=%async_computation.3 | async-start | bytes 2621440 | tf_op jit(solution)/shard_map/all_gather | solution.py:77
  269.2 8.9 %copy-start.3 = (f32[8,128,8,128]{3,1,2,0:T(8,128)S(1)}, f32[8,128,8,128]{3,1,2,0:T(8,128)}, u32[]{:S(2)}) copy-start(f32[8,128,8,128]{3,1,2,0:T(8,128)} %copy-done) | copy-start | bytes 12582916
  282.9 86.6 %all-gather.19.cloned.1.call-start = ((), (), s32[]{:S(2)}) async-start(), calls=%async_computation.4 | async-start | bytes 2621440 | tf_op jit(solution)/shard_map/all_gather | solution.py:77
  322.2 8.9 %copy-start.4 = (f32[8,128,8,128]{3,1,2,0:T(8,128)S(1)}, f32[8,128,8,128]{3,1,2,0:T(8,128)}, u32[]{:S(2)}) copy-start(f32[8,128,8,128]{3,1,2,0:T(8,128)} %copy-done) | copy-start | bytes 12582916
Sparse Core Ops, SparseCore 0:
  121.2 37.2 all-gather.10
  177.0 33.4 all-gather.12
  230.1 33.4 all-gather.14
  283.0 33.4 all-gather.16
  336.1 33.4 all-gather.18
